TPU v7x, 256 devices: a whole 4x4x8 slice. The times are simulated.
256 devices in a mesh: group: 8 (over z), member: 32 (over x, y, core).
Axes of the slice: x: 4, y: 4, z: 8, core: 2. Of those that a mesh axis runs over, the one named last changes fastest.
Arguments:
- diag_tiles: bfloat16 [4096, 4, 128, 128], P(('group', 'member')), may hold values from -0.21875 to 0.21875
- diag_cols: int32 [4096, 4], P(('group', 'member')), may hold values from 0 to 15
- offd_tiles: bfloat16 [4096, 2, 128, 128], P(('group', 'member')), may hold values from -0.21875 to 0.21875
- offd_cols: int32 [4096, 2], P(('group', 'member')), may hold values from 0 to 31, as said below
- offd_count: int32 [4096], P(('group', 'member')), may hold values from 0 to 2
- p_tiles: bfloat16 [4096, 2, 128, 128], P(('group', 'member')), may hold values from -2 to 2
- p_cols: int32 [4096, 2], P(('group', 'member')), may hold values from 0 to 255, as said below
- send_rows: int32 [256, 32, 1], P(('group', 'member')), may hold values from 0 to 15
- coarse_cols: int32 [256, 8], replicated, may hold values from 0 to 255, as said below
Outputs:
- coarse_tiles: float32 [256, 8, 128, 128], P(('group', 'member'))
Inputs may be any that keep to these rules, and one draw needn't show every extreme that they name: `p_cols`: the 2 entries of fine block row f on group g and member m are distinct coarse rows h * 32 + m with h one of g, (g + 1) % 8, (g + 4) % 8. `offd_cols`: A remote tile of a fine block row on member m reads a row sent by member (m - 1) % 32, (m + 1) % 32 or (m + 16) % 32. `coarse_cols`: the 8 entries of coarse row h * 32 + m are distinct; they are that row itself and the rows ((h + 1) % 8) * 32 + m, ((h - 1) % 8) * 32 + m, ((h + 4) % 8) * 32 + m, then four rows h2 * 32 + m2 with h2 among h - 1, h, h + 1, h + 4 and m2 among m - 1, m + 1, m + 32 // 2 (both modulo their counts).
All inputs are finite; a program needn't handle non-finite values.
Results may differ from a plain program's by a relative error of at most 0.005.
Values may be sent and summed in bfloat16 or wider, within the bound.
No kernel may reach another device: no remote copies, remote signals or barrier semaphores. Data moves between devices by JAX's collectives and lax.ppermute only.
A program may use at most 128 MiB of HBM per device.

v0:
```python
import functools

import jax
import jax.numpy as jnp
from jax import lax
from jax.experimental import pallas as pl
from jax.experimental.pallas import tpu as pltpu
from jax.sharding import PartitionSpec as P


T = 128
HDR = 32
BF = jnp.bfloat16
F32 = jnp.float32


def distance(column, group, groups, members):
    return ((column >> (members.bit_length() - 1)) - group) & (groups - 1)


def kind_of(column, group, groups, members):
    rel = distance(column, group, groups, members)
    return jnp.where(rel < 2, rel, jnp.where(rel == groups // 2, 2, 3))


def live_kind_of(column, group, groups, members):
    return jnp.minimum(distance(column, group, groups, members), 2)


def partners_of(member, members):
    odd = lax.rem(member, 2)
    up = lax.rem(member + 1, members)
    down = lax.rem(member + members - 1, members)
    return (
        jnp.where(odd == 1, down, up),
        jnp.where(odd == 1, up, down),
        lax.rem(member + members // 2, members),
    )


def fill_slots(slot_ref, pc_ref, rows, group, groups, members):
    for f in range(rows):
        for h in range(3):
            slot_ref[h, f] = 2 * rows
    for f in range(rows):
        for q in range(2):
            slot_ref[live_kind_of(pc_ref[q, f], group, groups, members), f] = 2 * f + q


def pick_kernel(
    groups, members, rows,
    send_hbm, pc_hbm, oc_hbm, cnt_hbm, dc_hbm, p_hbm,
    o0, o1, o2, pv, slot_ref, live_ref, dc_out,
    send_ref, pc_ref, oc_ref, cnt_ref, dc_ref, sems,
):
    group = lax.axis_index("group")
    partners = partners_of(lax.axis_index("member"), members)
    copies = [
        pltpu.make_async_copy(src, dst, sems.at[i])
        for i, (src, dst) in enumerate(
            (
                (send_hbm, send_ref),
                (pc_hbm, pc_ref),
                (p_hbm, pv.at[pl.ds(0, 2 * rows)]),
                (oc_hbm, oc_ref),
                (cnt_hbm, cnt_ref),
                (dc_hbm, dc_ref),
            )
        )
    ]
    for copy in copies:
        copy.start()
    pv[2 * rows] = jnp.zeros((T, T), BF)
    copies[0].wait()
    copies[1].wait()
    picked = [send_ref[0, partner] for partner in partners]
    for row, out in zip(picked, (o0, o1, o2)):
        for q in range(2):
            kind = live_kind_of(pc_ref[q, row], group, groups, members)
            at = 2 * T + q * (HDR // 2)
            out[at : at + HDR // 2, :] = jnp.full((HDR // 2, T), kind.astype(F32), F32).astype(BF)
    for copy in copies[3:]:
        copy.wait()
    fill_slots(slot_ref, pc_ref, rows, group, groups, members)
    for f in range(rows):
        for k in range(2):
            sender = oc_ref[k, f]
            e = jnp.where(sender == partners[0], 0, jnp.where(sender == partners[1], 1, 2))
            live_ref[k, f] = jnp.where(k < cnt_ref[f], e, 3)
        for k in range(4):
            dc_out[k, f] = dc_ref[k, f]
    copies[2].wait()
    for row, out in zip(picked, (o0, o1, o2)):
        out[0:T, :] = pv[2 * row]
        out[T : 2 * T, :] = pv[2 * row + 1]


def left_rows(pt, slot_ref, rows, h):
    return jnp.concatenate([pt[slot_ref[h, f]] for f in range(rows)], axis=1)


def remote_right(rows, aq):
    return jnp.concatenate(
        [jnp.concatenate([aq[f, e] for e in range(3)], axis=1) for f in range(rows)], axis=0
    )


def local_right(rows, z):
    return jnp.concatenate([z[f] for f in range(rows)], axis=0)


def split_into(out, qs):
    for e in range(3):
        block = qs[:, e * T : (e + 1) * T]
        high = block.astype(BF)
        out[e, :, 0:T] = high
        out[e, :, T : 2 * T] = (block - high.astype(F32)).astype(BF)


def local_kernel(rows, slot_ref, live_ref, dc_ref, pv, ov, dv, far_ref, q_ref, pt, aq, z):
    zero = jnp.zeros((T, T), BF)
    pt[2 * rows] = zero
    for t in range(2 * rows):
        pt[t] = pv[t].T
    for f in range(rows):
        a = jnp.concatenate([dv[f, k] for k in range(4)], axis=1)
        js = [dc_ref[k, f] for k in range(4)]
        b = jnp.concatenate(
            [jnp.concatenate([pv[slot_ref[h, j]] for h in range(3)], axis=1) for j in js], axis=0
        )
        z[f] = jnp.dot(a, b, preferred_element_type=F32).astype(BF)
        for e in range(3):
            aq[f, e] = lax.select(live_ref[0, f] == e, ov[f, 0], zero) + lax.select(
                live_ref[1, f] == e, ov[f, 1], zero
            )
    lhs = jnp.concatenate([left_rows(pt, slot_ref, rows, h) for h in (1, 2)], axis=0)
    qs = jnp.dot(lhs, remote_right(rows, aq), preferred_element_type=F32)
    gs = jnp.dot(lhs, local_right(rows, z), preferred_element_type=F32).astype(BF)
    for i in range(2):
        split_into(q_ref.at[i], qs[i * T : (i + 1) * T])
    for i, (h, c) in enumerate(((1, 1), (1, 0), (2, 2), (2, 0))):
        far_ref[i] = gs[(h - 1) * T : h * T, c * T : (c + 1) * T]


def received(pay_refs, rd):
    for e in range(3):
        kinds = [pay_refs[e][2 * T + 16 * q : 2 * T + 16 * q + 16, :].astype(F32) for q in range(2)]
        tiles = [pay_refs[e][q * T : (q + 1) * T, :].reshape(8, 16, T) for q in range(2)]
        for h in range(3):
            masks = [jnp.where(kind == h, 1.0, 0.0).astype(BF)[None] for kind in kinds]
            rd[3 * e + h] = (tiles[0] * masks[0] + tiles[1] * masks[1]).reshape(T, T)
    rd[9] = jnp.zeros((T, T), BF)


def remote_tile(groups, members, group, partners, cc_ref, left, rd, h, s):
    row = lax.rem(group + (0, 1, groups // 2)[h], groups) * members + lax.axis_index("member")
    col = cc_ref[4 + s, row]
    m2 = lax.rem(col, members)
    e = jnp.where(m2 == partners[0], 0, jnp.where(m2 == partners[1], 1, 2))
    kind = kind_of(col, group, groups, members)
    tile = rd[jnp.where(kind == 3, 9, 3 * e + kind)]
    return jnp.dot(left[e], jnp.concatenate([tile, tile], axis=0), preferred_element_type=F32)


def far_kernel(groups, members, cc_ref, far_ref, q_ref, r0, r1, r2, s1_ref, s4_ref, rd):
    group = lax.axis_index("group")
    partners = partners_of(lax.axis_index("member"), members)
    received((r0, r1, r2), rd)
    for h, out in ((2, s4_ref), (1, s1_ref)):
        out[0] = far_ref[2 * h - 2]
        out[1] = far_ref[2 * h - 1]
        for s in range(4):
            tile = remote_tile(
                groups, members, group, partners, cc_ref, q_ref.at[h - 1], rd, h, s
            )
            out[2 + s] = tile.astype(BF)


def near_kernel(
    groups, members, rows, cc_ref, slot_ref, pt, aq, z, r0, r1, r2, own_ref, rd, q_ref
):
    group = lax.axis_index("group")
    partners = partners_of(lax.axis_index("member"), members)
    received((r0, r1, r2), rd)
    lhs = left_rows(pt, slot_ref, rows, 0)
    split_into(q_ref, jnp.dot(lhs, remote_right(rows, aq), preferred_element_type=F32))
    near = jnp.dot(lhs, local_right(rows, z), preferred_element_type=F32)
    own_ref[0] = near[:, 0:T]
    own_ref[1] = near[:, T : 2 * T]
    own_ref[2] = jnp.zeros((T, T), F32)
    own_ref[3] = near[:, 2 * T : 3 * T]
    for s in range(4):
        own_ref[4 + s] = remote_tile(groups, members, group, partners, cc_ref, q_ref, rd, 0, s)


def add_kernel(own_ref, a1_ref, a4_ref, out_ref):
    out_ref[0, 0] = own_ref[0] + a1_ref[0].astype(F32) + a4_ref[0].astype(F32)
    out_ref[0, 1] = own_ref[1]
    out_ref[0, 2] = own_ref[2] + a1_ref[1].astype(F32)
    out_ref[0, 3] = own_ref[3] + a4_ref[1].astype(F32)
    for s in range(4):
        out_ref[0, 4 + s] = (
            own_ref[4 + s] + a1_ref[2 + s].astype(F32) + a4_ref[2 + s].astype(F32)
        )


def on_device(
    diag_tiles, diag_cols, offd_tiles, offd_cols, offd_count, p_tiles, p_cols, send_rows,
    coarse_cols,
):
    rows = p_tiles.shape[0]
    groups = lax.axis_size("group")
    members = lax.axis_size("member")
    vmem = pl.BlockSpec(memory_space=pltpu.VMEM)
    smem = pl.BlockSpec(memory_space=pltpu.SMEM)
    hbm = pl.BlockSpec(memory_space=pl.ANY)
    half = members // 2
    shift = groups // 2

    def inside(x):
        return pltpu.with_memory_space_constraint(x, pltpu.VMEM)

    def outside(x):
        return pltpu.with_memory_space_constraint(x, pltpu.HBM)

    def call(kernel, out_shape, in_specs, scratch, mib, mflop=10):
        return pl.pallas_call(
            kernel,
            out_shape=out_shape,
            in_specs=in_specs,
            out_specs=jax.tree.map(
                lambda x: pl.BlockSpec(memory_space=x.memory_space),
                out_shape,
                is_leaf=lambda x: not isinstance(x, tuple),
            ),
            scratch_shapes=scratch,
            compiler_params=pltpu.CompilerParams(vmem_limit_bytes=mib << 20),
            cost_estimate=pl.CostEstimate(
                flops=mflop * 10**6, transcendentals=0, bytes_accessed=mflop * 10**4
            ),
        )

    payload = pltpu.VMEM((2 * T + HDR, T), BF)
    *sends, pv, slot, live, dcols = call(
        functools.partial(pick_kernel, groups, members, rows),
        (
            payload, payload, payload, pltpu.VMEM((2 * rows + 1, T, T), BF),
            pltpu.SMEM((3, rows), jnp.int32),
            pltpu.SMEM((2, rows), jnp.int32),
            pltpu.SMEM((4, rows), jnp.int32),
        ),
        [hbm] * 6,
        [
            pltpu.SMEM((1, members), jnp.int32),
            pltpu.SMEM((2, rows), jnp.int32),
            pltpu.SMEM((2, rows), jnp.int32),
            pltpu.SMEM((rows,), jnp.int32),
            pltpu.SMEM((4, rows), jnp.int32),
            pltpu.SemaphoreType.DMA((6,)),
        ],
        8,
        2000,
    )(
        outside(send_rows.reshape(1, members)), outside(p_cols.T), outside(offd_cols.T),
        outside(offd_count), outside(diag_cols.T), outside(p_tiles.reshape(2 * rows, T, T)),
    )
    pairs = (
        [(i, i ^ 1) for i in range(members)],
        [(i, (i - 1 if i % 2 == 0 else i + 1) % members) for i in range(members)],
        [(i, (i + half) % members) for i in range(members)],
    )
    got = [None] * 3
    for e in (2, 1, 0):
        got[e] = inside(lax.ppermute(sends[e], "member", pairs[e]))

    far, qs, pt, aq, z = call(
        functools.partial(local_kernel, rows),
        (
            pltpu.VMEM((4, T, T), BF),
            pltpu.VMEM((2, 3, T, 2 * T), BF),
            pltpu.VMEM((2 * rows + 1, T, T), BF),
            pltpu.VMEM((rows, 3, T, T), BF),
            pltpu.VMEM((rows, T, 3 * T), BF),
        ),
        [smem] * 3 + [vmem] * 3,
        [],
        16,
        2000,
    )(slot, live, dcols, inside(pv), inside(offd_tiles), inside(diag_tiles))
    far, qs, pt, aq, z = [inside(x) for x in (far, qs, pt, aq, z)]

    def along_group(x, step):
        return inside(lax.ppermute(x, "group", [(i, (i + step) % groups) for i in range(groups)]))

    rd = pltpu.VMEM((10, T, T), BF)
    six = pltpu.VMEM((6, T, T), BF)
    ccols = outside(coarse_cols.T)
    send1, send4 = call(
        functools.partial(far_kernel, groups, members),
        (six, six), [smem] + [vmem] * 5, [rd], 8,
    )(ccols, far, qs, *got)
    a4 = along_group(send4, shift)
    a1 = along_group(send1, 1)
    own = call(
        functools.partial(near_kernel, groups, members, rows),
        pltpu.VMEM((8, T, T), F32), [smem] * 2 + [vmem] * 6,
        [rd, pltpu.VMEM((3, T, 2 * T), BF)], 12, 1000,
    )(ccols, slot, pt, aq, z, *got)
    return pl.pallas_call(
        add_kernel,
        out_shape=jax.ShapeDtypeStruct((1, 8, T, T), F32),
        in_specs=[vmem] * 3,
        out_specs=vmem,
        compiler_params=pltpu.CompilerParams(vmem_limit_bytes=8 << 20),
        name="add",
    )(inside(own), a1, a4)


def solution(mesh):
    return jax.shard_map(
        on_device,
        mesh=mesh,
        in_specs=(
            P(("group", "member"), None, None, None),
            P(("group", "member"), None),
            P(("group", "member"), None, None, None),
            P(("group", "member"), None),
            P(("group", "member")),
            P(("group", "member"), None, None, None),
            P(("group", "member"), None),
            P(("group", "member"), None, None),
            P(),
        ),
        out_specs=P(("group", "member"), None, None, None),
        check_vma=False,
    )
```

profile of v0, /device:TPU:31, one launch (start us, length us, event | category | flops | bytes accessed | tf_op | source)
XLA Modules:
  0.0 31.6 jit_solution(7575321406231203649)
XLA Ops:
  0.0 0.0 copy-start
  0.0 0.0 copy-start.1
  0.0 1.5 %shard_map.91 = (bf16[288,128]{1,0:T(8,128)(2,1)S(1)}, bf16[288,128]{1,0:T(8,128)(2,1)S(1)}, bf16[288,128]{1,0:T(8,128)(2,1)S(1)}, bf16[33,128,128]{2,1,0:T(8,12...) custom-call(s32[1,32]{1,0:T(1,128)} %bitcast.12, s32[2,16]{1,0:T(2,128)} %bitcast.10, ...), custom_call_target="tpu_custom_call" | custom-call | flops 2000000000 | bytes 20000000 | tf_op jit(solution)/shard_map/pallas_call | solution.py:244
  1.5 0.8 %collective-permute-start = (bf16[288,128]{1,0:T(8,128)(2,1)S(1)}, bf16[288,128]{1,0:T(8,128)(2,1)S(1)}, u32[]{:S(2)}, u32[]{:S(2)}) collective-permute-start(bf16[288,128]{1,0:T(8,128)(2,1)S(1)} %get-tuple-element.26), channel_id=1, source_target_pairs={{0,1},{1,0},{2,3},{3,2},{4,5},{5,4},{6,7},{7,6},{8,9},{9,8},{10,11... | collective-permute-start | bytes 221192 | tf_op jit(solution)/shard_map/ppermute | solution.py:274
  2.2 1.5 %collective-permute-start.1 = (bf16[288,128]{1,0:T(8,128)(2,1)S(1)}, bf16[288,128]{1,0:T(8,128)(2,1)S(1)}, u32[]{:S(2)}, u32[]{:S(2)}) collective-permute-start(bf16[288,128]{1,0:T(8,128)(2,1)S(1)} %get-tuple-element.27), channel_id=1, source_target_pairs={{0,31},{1,2},{2,1},{3,4},{4,3},{5,6},{6,5},{7,8},{8,7},{9,10},{10,... | collective-permute-start | bytes 221192 | tf_op jit(solution)/shard_map/ppermute | solution.py:274
  3.8 0.4 %collective-permute-start.2 = (bf16[288,128]{1,0:T(8,128)(2,1)S(1)}, bf16[288,128]{1,0:T(8,128)(2,1)S(1)}, u32[]{:S(2)}, u32[]{:S(2)}) collective-permute-start(bf16[288,128]{1,0:T(8,128)(2,1)S(1)} %get-tuple-element.28), channel_id=1, source_target_pairs={{0,16},{1,17},{2,18},{3,19},{4,20},{5,21},{6,22},{7,23},{8,24},{9,... | collective-permute-start | bytes 221192 | tf_op jit(solution)/shard_map/ppermute | solution.py:274
  4.2 0.0 copy-done
  4.2 0.0 copy-done.1
  4.2 2.7 %shard_map.92 = (bf16[4,128,128]{2,1,0:T(8,128)(2,1)S(1)}, bf16[2,3,128,256]{3,2,1,0:T(8,128)(2,1)S(1)}, bf16[33,128,128]{2,1,0:T(8,128)(2,1)S(1)}, bf16[16,3,12...) custom-call(s32[3,16]{1,0:T(4,128)S(4)} %get-tuple-element.19.slot_ref, s32[2,16]{1,0:T(2,128)S(4)} %get-tuple-element.20.live_ref, ...), custom_call_target="tpu_custom_call" | custom-call | flops 2000000000 | bytes 20000000 | tf_op jit(solution)/shard_map/pallas_call | solution.py:276
  7.0 0.0 collective-permute-done.r0
  7.0 2.4 %collective-permute-done.1.r1 = bf16[288,128]{1,0:T(8,128)(2,1)S(1)} collective-permute-done((bf16[288,128]{1,0:T(8,128)(2,1)S(1)}, bf16[288,128]{1,0:T(8,128)(2,1)S(1)}, u32[]{:S(2)}, u32[]{:S(2)}) %collective-permute-start.1) | collective-permute-done | bytes 73760 | tf_op jit(solution)/shard_map/ppermute | solution.py:274
  9.3 0.0 collective-permute-done.2.r2
  9.3 1.2 %shard_map.94 = (bf16[6,128,128]{2,1,0:T(8,128)(2,1)S(1)}, bf16[6,128,128]{2,1,0:T(8,128)(2,1)S(1)}) custom-call(s32[8,256]{1,0:T(8,128)} %bitcast.6, bf16[4,128,128]{2,1,0:T(8,128)(2,1)S(1)} %get-tuple-element.29.far_ref, bf16[2,3,128,256]{3,2,1,0:T(8,128)(2,1)S(1)} %get-tuple-element.30.q_ref, bf16[288,128]{1,0:T(8,128)(2,1)S(1)} %collective-permute-done.r0, ...), custom_call_target="tpu_custom_call" | custom-call | flops 10000000 | bytes 100000 | tf_op jit(solution)/shard_map/pallas_call | solution.py:298
  10.5 1.7 %collective-permute-start.3 = (bf16[6,128,128]{2,1,0:T(8,128)(2,1)S(1)}, bf16[6,128,128]{2,1,0:T(8,128)(2,1)S(1)}, u32[]{:S(2)}, u32[]{:S(2)}) collective-permute-start(bf16[6,128,128]{2,1,0:T(8,128)(2,1)S(1)} %get-tuple-element.31), channel_id=1, source_target_pairs={{0,32},{32,64},{64,96},{96,128},{128,160},{160,192},{192,224},{224... | collective-permute-start | bytes 589832 | tf_op jit(solution)/shard_map/ppermute | solution.py:293
  12.2 6.0 %collective-permute-start.4 = (bf16[6,128,128]{2,1,0:T(8,128)(2,1)S(1)}, bf16[6,128,128]{2,1,0:T(8,128)(2,1)S(1)}, u32[]{:S(2)}, u32[]{:S(2)}) collective-permute-start(bf16[6,128,128]{2,1,0:T(8,128)(2,1)S(1)} %get-tuple-element.32), channel_id=1, source_target_pairs={{0,128},{32,160},{64,192},{96,224},{128,0},{160,32},{192,64},{224,... | collective-permute-start | bytes 589832 | tf_op jit(solution)/shard_map/ppermute | solution.py:293
  18.2 1.6 %shard_map.93.own_ref = f32[8,128,128]{2,1,0:T(8,128)S(1)} custom-call(s32[8,256]{1,0:T(8,128)} %bitcast.7, s32[3,16]{1,0:T(4,128)S(4)} %get-tuple-element.19.slot_ref, bf16[33,128,128]{2,1,0:T(8,128)(2,1)S(1)} %get-tuple-element.23.pt, bf16[16,3,128,128]{3,2,1,0:T(8,128)(2,1)S(1)} %get-tuple-element.24.aq, bf16[16,128,384]{2,1,0:T(8,128)(2,1)S(1)} %get-tuple-element.25.z, ...), custom_call_target="tpu_custom_call" | custom-call | flops 1000000000 | bytes 10000000 | tf_op jit(solution)/shard_map/pallas_call | solution.py:304
  19.8 1.4 %collective-permute-done.3.a1_ref = bf16[6,128,128]{2,1,0:T(8,128)(2,1)S(1)} collective-permute-done((bf16[6,128,128]{2,1,0:T(8,128)(2,1)S(1)}, bf16[6,128,128]{2,1,0:T(8,128)(2,1)S(1)}, u32[]{:S(2)}, u32[]{:S(2)}) %collective-permute-start.3) | collective-permute-done | bytes 196640 | tf_op jit(solution)/shard_map/ppermute | solution.py:293
  21.2 9.5 %collective-permute-done.4.a4_ref = bf16[6,128,128]{2,1,0:T(8,128)(2,1)S(1)} collective-permute-done((bf16[6,128,128]{2,1,0:T(8,128)(2,1)S(1)}, bf16[6,128,128]{2,1,0:T(8,128)(2,1)S(1)}, u32[]{:S(2)}, u32[]{:S(2)}) %collective-permute-start.4) | collective-permute-done | bytes 196640 | tf_op jit(solution)/shard_map/ppermute | solution.py:293
  30.7 0.9 %add.1 = f32[1,8,128,128]{3,2,1,0:T(8,128)} custom-call(f32[8,128,128]{2,1,0:T(8,128)S(1)} %shard_map.93.own_ref, bf16[6,128,128]{2,1,0:T(8,128)(2,1)S(1)} %collective-permute-done.3.a1_ref, bf16[6,128,128]{2,1,0:T(8,128)(2,1)S(1)} %collective-permute-done.4.a4_ref), custom_call_target="tpu_custom_call" | custom-call | tf_op jit(solution)/shard_map/add/pallas_call | solution.py:309
Async XLA Ops:
  0.0 4.2 %copy-start = (bf16[16,4,128,128]{3,2,1,0:T(8,128)(2,1)S(1)}, bf16[16,4,128,128]{3,2,1,0:T(8,128)(2,1)}, u32[]{:S(2)}) copy-start(bf16[16,4,128,128]{3,2,1,0:T(8,128)(2,1)} %dv.1) | copy-start | bytes 6291460
  0.0 4.2 %copy-start.1 = (bf16[16,2,128,128]{3,2,1,0:T(8,128)(2,1)S(1)}, bf16[16,2,128,128]{3,2,1,0:T(8,128)(2,1)}, u32[]{:S(2)}) copy-start(bf16[16,2,128,128]{3,2,1,0:T(8,128)(2,1)} %ov.1) | copy-start | bytes 3145732
  1.5 5.5 %collective-permute-start = (bf16[288,128]{1,0:T(8,128)(2,1)S(1)}, bf16[288,128]{1,0:T(8,128)(2,1)S(1)}, u32[]{:S(2)}, u32[]{:S(2)}) collective-permute-start(bf16[288,128]{1,0:T(8,128)(2,1)S(1)} %get-tuple-element.26), channel_id=1, source_target_pairs={{0,1},{1,0},{2,3},{3,2},{4,5},{5,4},{6,7},{7,6},{8,9},{9,8},{10,11... | collective-permute-start | bytes 221192 | tf_op jit(solution)/shard_map/ppermute | solution.py:274
  2.2 7.1 %collective-permute-start.1 = (bf16[288,128]{1,0:T(8,128)(2,1)S(1)}, bf16[288,128]{1,0:T(8,128)(2,1)S(1)}, u32[]{:S(2)}, u32[]{:S(2)}) collective-permute-start(bf16[288,128]{1,0:T(8,128)(2,1)S(1)} %get-tuple-element.27), channel_id=1, source_target_pairs={{0,31},{1,2},{2,1},{3,4},{4,3},{5,6},{6,5},{7,8},{8,7},{9,10},{10,... | collective-permute-start | bytes 221192 | tf_op jit(solution)/shard_map/ppermute | solution.py:274
  3.8 5.6 %collective-permute-start.2 = (bf16[288,128]{1,0:T(8,128)(2,1)S(1)}, bf16[288,128]{1,0:T(8,128)(2,1)S(1)}, u32[]{:S(2)}, u32[]{:S(2)}) collective-permute-start(bf16[288,128]{1,0:T(8,128)(2,1)S(1)} %get-tuple-element.28), channel_id=1, source_target_pairs={{0,16},{1,17},{2,18},{3,19},{4,20},{5,21},{6,22},{7,23},{8,24},{9,... | collective-permute-start | bytes 221192 | tf_op jit(solution)/shard_map/ppermute | solution.py:274
  10.5 10.7 %collective-permute-start.3 = (bf16[6,128,128]{2,1,0:T(8,128)(2,1)S(1)}, bf16[6,128,128]{2,1,0:T(8,128)(2,1)S(1)}, u32[]{:S(2)}, u32[]{:S(2)}) collective-permute-start(bf16[6,128,128]{2,1,0:T(8,128)(2,1)S(1)} %get-tuple-element.31), channel_id=1, source_target_pairs={{0,32},{32,64},{64,96},{96,128},{128,160},{160,192},{192,224},{224... | collective-permute-start | bytes 589832 | tf_op jit(solution)/shard_map/ppermute | solution.py:293
  12.2 18.5 %collective-permute-start.4 = (bf16[6,128,128]{2,1,0:T(8,128)(2,1)S(1)}, bf16[6,128,128]{2,1,0:T(8,128)(2,1)S(1)}, u32[]{:S(2)}, u32[]{:S(2)}) collective-permute-start(bf16[6,128,128]{2,1,0:T(8,128)(2,1)S(1)} %get-tuple-element.32), channel_id=1, source_target_pairs={{0,128},{32,160},{64,192},{96,224},{128,0},{160,32},{192,64},{224,... | collective-permute-start | bytes 589832 | tf_op jit(solution)/shard_map/ppermute | solution.py:293
where the time goes:
time: 31.8 us; the launch traced here: 31.6 us
  waiting for transfers between devices  13.3 us (42%)
  starting transfers between devices  10.5 us (33%)
  Pallas kernels  7.81 us (25%)
    ppermute x2, waiting for transfers between devices, along_group(): lax.ppermute(x, 'group', [(i, (i + step) % groups) for i in range(groups)])  10.9 us
    ppermute x2, starting transfers between devices, along_group(): lax.ppermute(x, 'group', [(i, (i + step) % groups) for i in range(groups)])  7.72 us
    ppermute x3, starting transfers between devices, on_device(): got[e] = inside(lax.ppermute(sends[e], 'member', pairs[e]))  2.74 us
    pallas_call x1, Pallas kernels, on_device(): call(functools.partial(local_kernel, rows), (pltpu.VMEM((4, T, T), BF), p...  2.74 us
    ppermute x3, waiting for transfers between devices, on_device(): got[e] = inside(lax.ppermute(sends[e], 'member', pairs[e]))  2.36 us
    pallas_call x1, Pallas kernels, on_device(): call(functools.partial(near_kernel, groups, members, rows), pltpu.VMEM((8...  1.59 us
    pallas_call x1, Pallas kernels, on_device(): call(functools.partial(pick_kernel, groups, members, rows), (payload, pay...  1.45 us
    pallas_call x1, Pallas kernels, on_device(): call(functools.partial(far_kernel, groups, members), (six, six), [smem] +...  1.17 us
  transfers between devices with their start and end apart: 5, of which 3 were waited for; matrix products, arithmetic and copies ran while one was open for 0% of the time, Pallas kernels for 14%

commit v1 on v0

--- a/solution.py
+++ b/solution.py
@@ -49,9 +49,9 @@
 
 def pick_kernel(
     groups, members, rows,
-    send_hbm, pc_hbm, oc_hbm, cnt_hbm, dc_hbm, p_hbm,
-    o0, o1, o2, pv, slot_ref, live_ref, dc_out,
-    send_ref, pc_ref, oc_ref, cnt_ref, dc_ref, sems,
+    send_hbm, pc_hbm, oc_hbm, cnt_hbm, dc_hbm, cc_hbm, p_hbm,
+    o0, o1, o2, pv, slot_ref, live_ref, dc_out, pick_ref,
+    send_ref, pc_ref, oc_ref, cnt_ref, dc_ref, cc_ref, sems,
 ):
     group = lax.axis_index("group")
     partners = partners_of(lax.axis_index("member"), members)
@@ -65,6 +65,7 @@
                 (oc_hbm, oc_ref),
                 (cnt_hbm, cnt_ref),
                 (dc_hbm, dc_ref),
+                (cc_hbm, cc_ref),
             )
         )
     ]
@@ -89,6 +90,15 @@
             live_ref[k, f] = jnp.where(k < cnt_ref[f], e, 3)
         for k in range(4):
             dc_out[k, f] = dc_ref[k, f]
+    for h in range(3):
+        target = ((group + (0, 1, groups // 2)[h]) & (groups - 1)) * members
+        for s in range(4):
+            col = cc_ref[4 + s, target + lax.axis_index("member")]
+            m2 = col & (members - 1)
+            e = jnp.where(m2 == partners[0], 0, jnp.where(m2 == partners[1], 1, 2))
+            kind = kind_of(col, group, groups, members)
+            pick_ref[2 * h, s] = e
+            pick_ref[2 * h + 1, s] = jnp.where(kind == 3, 9, 3 * e + kind)
     copies[2].wait()
     for row, out in zip(picked, (o0, o1, o2)):
         out[0:T, :] = pv[2 * row]
@@ -152,35 +162,25 @@
     rd[9] = jnp.zeros((T, T), BF)
 
 
-def remote_tile(groups, members, group, partners, cc_ref, left, rd, h, s):
-    row = lax.rem(group + (0, 1, groups // 2)[h], groups) * members + lax.axis_index("member")
-    col = cc_ref[4 + s, row]
-    m2 = lax.rem(col, members)
-    e = jnp.where(m2 == partners[0], 0, jnp.where(m2 == partners[1], 1, 2))
-    kind = kind_of(col, group, groups, members)
-    tile = rd[jnp.where(kind == 3, 9, 3 * e + kind)]
-    return jnp.dot(left[e], jnp.concatenate([tile, tile], axis=0), preferred_element_type=F32)
-
-
-def far_kernel(groups, members, cc_ref, far_ref, q_ref, r0, r1, r2, s1_ref, s4_ref, rd):
-    group = lax.axis_index("group")
-    partners = partners_of(lax.axis_index("member"), members)
+def remote_tile(pick_ref, left, rd, h, s):
+    tile = rd[pick_ref[2 * h + 1, s]]
+    return jnp.dot(
+        left[pick_ref[2 * h, s]],
+        jnp.concatenate([tile, tile], axis=0),
+        preferred_element_type=F32,
+    )
+
+
+def far_kernel(pick_ref, far_ref, q_ref, r0, r1, r2, s1_ref, s4_ref, rd):
     received((r0, r1, r2), rd)
     for h, out in ((2, s4_ref), (1, s1_ref)):
         out[0] = far_ref[2 * h - 2]
         out[1] = far_ref[2 * h - 1]
         for s in range(4):
-            tile = remote_tile(
-                groups, members, group, partners, cc_ref, q_ref.at[h - 1], rd, h, s
-            )
-            out[2 + s] = tile.astype(BF)
-
-
-def near_kernel(
-    groups, members, rows, cc_ref, slot_ref, pt, aq, z, r0, r1, r2, own_ref, rd, q_ref
-):
-    group = lax.axis_index("group")
-    partners = partners_of(lax.axis_index("member"), members)
+            out[2 + s] = remote_tile(pick_ref, q_ref.at[h - 1], rd, h, s).astype(BF)
+
+
+def near_kernel(rows, pick_ref, slot_ref, pt, aq, z, r0, r1, r2, own_ref, rd, q_ref):
     received((r0, r1, r2), rd)
     lhs = left_rows(pt, slot_ref, rows, 0)
     split_into(q_ref, jnp.dot(lhs, remote_right(rows, aq), preferred_element_type=F32))
@@ -190,7 +190,7 @@
     own_ref[2] = jnp.zeros((T, T), F32)
     own_ref[3] = near[:, 2 * T : 3 * T]
     for s in range(4):
-        own_ref[4 + s] = remote_tile(groups, members, group, partners, cc_ref, q_ref, rd, 0, s)
+        own_ref[4 + s] = remote_tile(pick_ref, q_ref, rd, 0, s)
 
 
 def add_kernel(own_ref, a1_ref, a4_ref, out_ref):
@@ -241,28 +241,31 @@
         )
 
     payload = pltpu.VMEM((2 * T + HDR, T), BF)
-    *sends, pv, slot, live, dcols = call(
+    *sends, pv, slot, live, dcols, chosen = call(
         functools.partial(pick_kernel, groups, members, rows),
         (
             payload, payload, payload, pltpu.VMEM((2 * rows + 1, T, T), BF),
             pltpu.SMEM((3, rows), jnp.int32),
             pltpu.SMEM((2, rows), jnp.int32),
             pltpu.SMEM((4, rows), jnp.int32),
+            pltpu.SMEM((6, 4), jnp.int32),
         ),
-        [hbm] * 6,
+        [hbm] * 7,
         [
             pltpu.SMEM((1, members), jnp.int32),
             pltpu.SMEM((2, rows), jnp.int32),
             pltpu.SMEM((2, rows), jnp.int32),
             pltpu.SMEM((rows,), jnp.int32),
             pltpu.SMEM((4, rows), jnp.int32),
-            pltpu.SemaphoreType.DMA((6,)),
+            pltpu.SMEM(coarse_cols.shape[::-1], jnp.int32),
+            pltpu.SemaphoreType.DMA((7,)),
         ],
         8,
         2000,
     )(
         outside(send_rows.reshape(1, members)), outside(p_cols.T), outside(offd_cols.T),
-        outside(offd_count), outside(diag_cols.T), outside(p_tiles.reshape(2 * rows, T, T)),
+        outside(offd_count), outside(diag_cols.T), outside(coarse_cols.T),
+        outside(p_tiles.reshape(2 * rows, T, T)),
     )
     pairs = (
         [(i, i ^ 1) for i in range(members)],
@@ -294,18 +297,17 @@
 
     rd = pltpu.VMEM((10, T, T), BF)
     six = pltpu.VMEM((6, T, T), BF)
-    ccols = outside(coarse_cols.T)
     send1, send4 = call(
-        functools.partial(far_kernel, groups, members),
+        far_kernel,
         (six, six), [smem] + [vmem] * 5, [rd], 8,
-    )(ccols, far, qs, *got)
+    )(chosen, far, qs, *got)
     a4 = along_group(send4, shift)
     a1 = along_group(send1, 1)
     own = call(
-        functools.partial(near_kernel, groups, members, rows),
+        functools.partial(near_kernel, rows),
         pltpu.VMEM((8, T, T), F32), [smem] * 2 + [vmem] * 6,
         [rd, pltpu.VMEM((3, T, 2 * T), BF)], 12, 1000,
-    )(ccols, slot, pt, aq, z, *got)
+    )(chosen, slot, pt, aq, z, *got)
     return pl.pallas_call(
         add_kernel,
         out_shape=jax.ShapeDtypeStruct((1, 8, T, T), F32),

time: 31.8 us -> 30.9 us (0.972)
  Pallas kernels: 7.81 us -> 6.24 us
  waiting for transfers between devices: 13.3 us -> 14.1 us
    pallas_call x2, Pallas kernels: 2.76 us -> 1.19 us  [the longest x1 0.81 us: on_device(): call(functools.partial(near_kernel, rows), pltpu.VMEM((8, T, T), F32), [s...]
    ppermute x2, waiting for transfers between devices: 10.9 us -> 11.7 us  [along_group(): lax.ppermute(x, 'group', [(i, (i + step) % groups) for i in range(groups)])]
  transfers between devices with their start and end apart: 5 -> 5, of which waited for: 3 -> 3; matrix products, arithmetic and copies ran while one was open for 0% -> 0% of each run, Pallas kernels for 14% -> 12%
where the time goes in v1:
time: 30.9 us; the launch traced here: 30.8 us
  waiting for transfers between devices  14.1 us (46%)
  starting transfers between devices  10.5 us (34%)
  Pallas kernels  6.24 us (20%)
    ppermute x2, waiting for transfers between devices, along_group(): lax.ppermute(x, 'group', [(i, (i + step) % groups) for i in range(groups)])  11.7 us
    ppermute x2, starting transfers between devices, along_group(): lax.ppermute(x, 'group', [(i, (i + step) % groups) for i in range(groups)])  7.72 us
    ppermute x3, starting transfers between devices, on_device(): got[e] = inside(lax.ppermute(sends[e], 'member', pairs[e]))  2.74 us
    pallas_call x1, Pallas kernels, on_device(): call(functools.partial(local_kernel, rows), (pltpu.VMEM((4, T, T), BF), p...  2.74 us
    ppermute x3, waiting for transfers between devices, on_device(): got[e] = inside(lax.ppermute(sends[e], 'member', pairs[e]))  2.36 us
    pallas_call x1, Pallas kernels, on_device(): call(functools.partial(pick_kernel, groups, members, rows), (payload, pay...  1.46 us
    pallas_call x1, Pallas kernels, on_device(): pl.pallas_call(add_kernel, out_shape=jax.ShapeDtypeStruct((1, 8, T, T), F...  0.85 us
    pallas_call x1, Pallas kernels, on_device(): call(functools.partial(near_kernel, rows), pltpu.VMEM((8, T, T), F32), [s...  0.81 us
  transfers between devices with their start and end apart: 5, of which 3 were waited for; matrix products, arithmetic and copies ran while one was open for 0% of the time, Pallas kernels for 12%

profile of v1, /device:TPU:31, one launch (start us, length us, event | category | flops | bytes accessed | tf_op | source)
XLA Modules:
  0.0 30.8 jit_solution(1762974186079989834)
XLA Ops:
  0.0 0.0 copy-start
  0.0 0.0 copy-start.1
  0.0 1.5 %shard_map.91 = (bf16[288,128]{1,0:T(8,128)(2,1)S(1)}, bf16[288,128]{1,0:T(8,128)(2,1)S(1)}, bf16[288,128]{1,0:T(8,128)(2,1)S(1)}, bf16[33,128,128]{2,1,0:T(8,12...) custom-call(s32[1,32]{1,0:T(1,128)} %bitcast.11, ...), custom_call_target="tpu_custom_call" | custom-call | flops 2000000000 | bytes 20000000 | tf_op jit(solution)/shard_map/pallas_call | solution.py:244
  1.5 0.8 %collective-permute-start = (bf16[288,128]{1,0:T(8,128)(2,1)S(1)}, bf16[288,128]{1,0:T(8,128)(2,1)S(1)}, u32[]{:S(2)}, u32[]{:S(2)}) collective-permute-start(bf16[288,128]{1,0:T(8,128)(2,1)S(1)} %get-tuple-element.28), channel_id=1, source_target_pairs={{0,1},{1,0},{2,3},{3,2},{4,5},{5,4},{6,7},{7,6},{8,9},{9,8},{10,11... | collective-permute-start | bytes 221192 | tf_op jit(solution)/shard_map/ppermute | solution.py:277
  2.2 1.5 %collective-permute-start.1 = (bf16[288,128]{1,0:T(8,128)(2,1)S(1)}, bf16[288,128]{1,0:T(8,128)(2,1)S(1)}, u32[]{:S(2)}, u32[]{:S(2)}) collective-permute-start(bf16[288,128]{1,0:T(8,128)(2,1)S(1)} %get-tuple-element.29), channel_id=1, source_target_pairs={{0,31},{1,2},{2,1},{3,4},{4,3},{5,6},{6,5},{7,8},{8,7},{9,10},{10,... | collective-permute-start | bytes 221192 | tf_op jit(solution)/shard_map/ppermute | solution.py:277
  3.8 0.4 %collective-permute-start.2 = (bf16[288,128]{1,0:T(8,128)(2,1)S(1)}, bf16[288,128]{1,0:T(8,128)(2,1)S(1)}, u32[]{:S(2)}, u32[]{:S(2)}) collective-permute-start(bf16[288,128]{1,0:T(8,128)(2,1)S(1)} %get-tuple-element.30), channel_id=1, source_target_pairs={{0,16},{1,17},{2,18},{3,19},{4,20},{5,21},{6,22},{7,23},{8,24},{9,... | collective-permute-start | bytes 221192 | tf_op jit(solution)/shard_map/ppermute | solution.py:277
  4.2 0.0 copy-done
  4.2 0.0 copy-done.1
  4.2 2.7 %shard_map.92 = (bf16[4,128,128]{2,1,0:T(8,128)(2,1)S(1)}, bf16[2,3,128,256]{3,2,1,0:T(8,128)(2,1)S(1)}, bf16[33,128,128]{2,1,0:T(8,128)(2,1)S(1)}, bf16[16,3,12...) custom-call(s32[3,16]{1,0:T(4,128)S(4)} %get-tuple-element.21.slot_ref, s32[2,16]{1,0:T(2,128)S(4)} %get-tuple-element.22.live_ref, ...), custom_call_target="tpu_custom_call" | custom-call | flops 2000000000 | bytes 20000000 | tf_op jit(solution)/shard_map/pallas_call | solution.py:279
  7.0 0.0 collective-permute-done.r0
  7.0 2.4 %collective-permute-done.1.r1 = bf16[288,128]{1,0:T(8,128)(2,1)S(1)} collective-permute-done((bf16[288,128]{1,0:T(8,128)(2,1)S(1)}, bf16[288,128]{1,0:T(8,128)(2,1)S(1)}, u32[]{:S(2)}, u32[]{:S(2)}) %collective-permute-start.1) | collective-permute-done | bytes 73760 | tf_op jit(solution)/shard_map/ppermute | solution.py:277
  9.3 0.0 collective-permute-done.2.r2
  9.3 0.4 %shard_map.94 = (bf16[6,128,128]{2,1,0:T(8,128)(2,1)S(1)}, bf16[6,128,128]{2,1,0:T(8,128)(2,1)S(1)}) custom-call(s32[6,4]{1,0:T(8,128)S(4)} %get-tuple-element.20.pick_ref, bf16[4,128,128]{2,1,0:T(8,128)(2,1)S(1)} %get-tuple-element.31.far_ref, bf16[2,3,128,256]{3,2,1,0:T(8,128)(2,1)S(1)} %get-tuple-element.32.q_ref, ...), custom_call_target="tpu_custom_call" | custom-call | flops 10000000 | bytes 100000 | tf_op jit(solution)/shard_map/pallas_call | solution.py:300
  9.7 1.7 %collective-permute-start.3 = (bf16[6,128,128]{2,1,0:T(8,128)(2,1)S(1)}, bf16[6,128,128]{2,1,0:T(8,128)(2,1)S(1)}, u32[]{:S(2)}, u32[]{:S(2)}) collective-permute-start(bf16[6,128,128]{2,1,0:T(8,128)(2,1)S(1)} %get-tuple-element.33), channel_id=1, source_target_pairs={{0,32},{32,64},{64,96},{96,128},{128,160},{160,192},{192,224},{224... | collective-permute-start | bytes 589832 | tf_op jit(solution)/shard_map/ppermute | solution.py:296
  11.4 6.0 %collective-permute-start.4 = (bf16[6,128,128]{2,1,0:T(8,128)(2,1)S(1)}, bf16[6,128,128]{2,1,0:T(8,128)(2,1)S(1)}, u32[]{:S(2)}, u32[]{:S(2)}) collective-permute-start(bf16[6,128,128]{2,1,0:T(8,128)(2,1)S(1)} %get-tuple-element.34), channel_id=1, source_target_pairs={{0,128},{32,160},{64,192},{96,224},{128,0},{160,32},{192,64},{224,... | collective-permute-start | bytes 589832 | tf_op jit(solution)/shard_map/ppermute | solution.py:296
  17.5 0.8 %shard_map.93.own_ref = f32[8,128,128]{2,1,0:T(8,128)S(1)} custom-call(s32[6,4]{1,0:T(8,128)S(4)} %get-tuple-element.20.pick_ref, s32[3,16]{1,0:T(4,128)S(4)} %get-tuple-element.21.slot_ref, bf16[33,128,128]{2,1,0:T(8,128)(2,1)S(1)} %get-tuple-element.25.pt, bf16[16,3,128,128]{3,2,1,0:T(8,128)(2,1)S(1)} %get-tuple-element.26.aq, ...), custom_call_target="tpu_custom_call" | custom-call | flops 1000000000 | bytes 10000000 | tf_op jit(solution)/shard_map/pallas_call | solution.py:306
  18.3 2.2 %collective-permute-done.3.a1_ref = bf16[6,128,128]{2,1,0:T(8,128)(2,1)S(1)} collective-permute-done((bf16[6,128,128]{2,1,0:T(8,128)(2,1)S(1)}, bf16[6,128,128]{2,1,0:T(8,128)(2,1)S(1)}, u32[]{:S(2)}, u32[]{:S(2)}) %collective-permute-start.3) | collective-permute-done | bytes 196640 | tf_op jit(solution)/shard_map/ppermute | solution.py:296
  20.4 9.5 %collective-permute-done.4.a4_ref = bf16[6,128,128]{2,1,0:T(8,128)(2,1)S(1)} collective-permute-done((bf16[6,128,128]{2,1,0:T(8,128)(2,1)S(1)}, bf16[6,128,128]{2,1,0:T(8,128)(2,1)S(1)}, u32[]{:S(2)}, u32[]{:S(2)}) %collective-permute-start.4) | collective-permute-done | bytes 196640 | tf_op jit(solution)/shard_map/ppermute | solution.py:296
  30.0 0.9 %add.1 = f32[1,8,128,128]{3,2,1,0:T(8,128)} custom-call(f32[8,128,128]{2,1,0:T(8,128)S(1)} %shard_map.93.own_ref, bf16[6,128,128]{2,1,0:T(8,128)(2,1)S(1)} %collective-permute-done.3.a1_ref, bf16[6,128,128]{2,1,0:T(8,128)(2,1)S(1)} %collective-permute-done.4.a4_ref), custom_call_target="tpu_custom_call" | custom-call | tf_op jit(solution)/shard_map/add/pallas_call | solution.py:311
Async XLA Ops:
  0.0 4.2 %copy-start = (bf16[16,4,128,128]{3,2,1,0:T(8,128)(2,1)S(1)}, bf16[16,4,128,128]{3,2,1,0:T(8,128)(2,1)}, u32[]{:S(2)}) copy-start(bf16[16,4,128,128]{3,2,1,0:T(8,128)(2,1)} %dv.1) | copy-start | bytes 6291460
  0.0 4.2 %copy-start.1 = (bf16[16,2,128,128]{3,2,1,0:T(8,128)(2,1)S(1)}, bf16[16,2,128,128]{3,2,1,0:T(8,128)(2,1)}, u32[]{:S(2)}) copy-start(bf16[16,2,128,128]{3,2,1,0:T(8,128)(2,1)} %ov.1) | copy-start | bytes 3145732
  1.5 5.5 %collective-permute-start = (bf16[288,128]{1,0:T(8,128)(2,1)S(1)}, bf16[288,128]{1,0:T(8,128)(2,1)S(1)}, u32[]{:S(2)}, u32[]{:S(2)}) collective-permute-start(bf16[288,128]{1,0:T(8,128)(2,1)S(1)} %get-tuple-element.28), channel_id=1, source_target_pairs={{0,1},{1,0},{2,3},{3,2},{4,5},{5,4},{6,7},{7,6},{8,9},{9,8},{10,11... | collective-permute-start | bytes 221192 | tf_op jit(solution)/shard_map/ppermute | solution.py:277
  2.2 7.1 %collective-permute-start.1 = (bf16[288,128]{1,0:T(8,128)(2,1)S(1)}, bf16[288,128]{1,0:T(8,128)(2,1)S(1)}, u32[]{:S(2)}, u32[]{:S(2)}) collective-permute-start(bf16[288,128]{1,0:T(8,128)(2,1)S(1)} %get-tuple-element.29), channel_id=1, source_target_pairs={{0,31},{1,2},{2,1},{3,4},{4,3},{5,6},{6,5},{7,8},{8,7},{9,10},{10,... | collective-permute-start | bytes 221192 | tf_op jit(solution)/shard_map/ppermute | solution.py:277
  3.8 5.6 %collective-permute-start.2 = (bf16[288,128]{1,0:T(8,128)(2,1)S(1)}, bf16[288,128]{1,0:T(8,128)(2,1)S(1)}, u32[]{:S(2)}, u32[]{:S(2)}) collective-permute-start(bf16[288,128]{1,0:T(8,128)(2,1)S(1)} %get-tuple-element.30), channel_id=1, source_target_pairs={{0,16},{1,17},{2,18},{3,19},{4,20},{5,21},{6,22},{7,23},{8,24},{9,... | collective-permute-start | bytes 221192 | tf_op jit(solution)/shard_map/ppermute | solution.py:277
  9.7 10.7 %collective-permute-start.3 = (bf16[6,128,128]{2,1,0:T(8,128)(2,1)S(1)}, bf16[6,128,128]{2,1,0:T(8,128)(2,1)S(1)}, u32[]{:S(2)}, u32[]{:S(2)}) collective-permute-start(bf16[6,128,128]{2,1,0:T(8,128)(2,1)S(1)} %get-tuple-element.33), channel_id=1, source_target_pairs={{0,32},{32,64},{64,96},{96,128},{128,160},{160,192},{192,224},{224... | collective-permute-start | bytes 589832 | tf_op jit(solution)/shard_map/ppermute | solution.py:296
  11.4 18.5 %collective-permute-start.4 = (bf16[6,128,128]{2,1,0:T(8,128)(2,1)S(1)}, bf16[6,128,128]{2,1,0:T(8,128)(2,1)S(1)}, u32[]{:S(2)}, u32[]{:S(2)}) collective-permute-start(bf16[6,128,128]{2,1,0:T(8,128)(2,1)S(1)} %get-tuple-element.34), channel_id=1, source_target_pairs={{0,128},{32,160},{64,192},{96,224},{128,0},{160,32},{192,64},{224,... | collective-permute-start | bytes 589832 | tf_op jit(solution)/shard_map/ppermute | solution.py:296

commit v2 on v1

--- a/solution.py
+++ b/solution.py
@@ -40,9 +40,6 @@
 
 def fill_slots(slot_ref, pc_ref, rows, group, groups, members):
     for f in range(rows):
-        for h in range(3):
-            slot_ref[h, f] = 2 * rows
-    for f in range(rows):
         for q in range(2):
             slot_ref[live_kind_of(pc_ref[q, f], group, groups, members), f] = 2 * f + q
 
@@ -50,8 +47,8 @@
 def pick_kernel(
     groups, members, rows,
     send_hbm, pc_hbm, oc_hbm, cnt_hbm, dc_hbm, cc_hbm, p_hbm,
-    o0, o1, o2, pv, slot_ref, live_ref, dc_out, pick_ref,
-    send_ref, pc_ref, oc_ref, cnt_ref, dc_ref, cc_ref, sems,
+    o0, o1, o2, pv, slot_ref, live_ref, dc_out, pick_ref, place_ref,
+    send_ref, pc_ref, oc_ref, cnt_ref, cc_ref, sems,
 ):
     group = lax.axis_index("group")
     partners = partners_of(lax.axis_index("member"), members)
@@ -64,7 +61,7 @@
                 (p_hbm, pv.at[pl.ds(0, 2 * rows)]),
                 (oc_hbm, oc_ref),
                 (cnt_hbm, cnt_ref),
-                (dc_hbm, dc_ref),
+                (dc_hbm, dc_out),
                 (cc_hbm, cc_ref),
             )
         )
@@ -72,6 +69,9 @@
     for copy in copies:
         copy.start()
     pv[2 * rows] = jnp.zeros((T, T), BF)
+    for f in range(rows):
+        for h in range(3):
+            slot_ref[h, f] = 2 * rows
     copies[0].wait()
     copies[1].wait()
     picked = [send_ref[0, partner] for partner in partners]
@@ -88,17 +88,22 @@
             sender = oc_ref[k, f]
             e = jnp.where(sender == partners[0], 0, jnp.where(sender == partners[1], 1, 2))
             live_ref[k, f] = jnp.where(k < cnt_ref[f], e, 3)
-        for k in range(4):
-            dc_out[k, f] = dc_ref[k, f]
+    member = lax.axis_index("member")
     for h in range(3):
-        target = ((group + (0, 1, groups // 2)[h]) & (groups - 1)) * members
-        for s in range(4):
-            col = cc_ref[4 + s, target + lax.axis_index("member")]
+        target = ((group + (0, 1, groups // 2)[h]) & (groups - 1)) * members + member
+        rank = jnp.int32(0)
+        for s in range(cc_ref.shape[0]):
+            col = cc_ref[s, target]
             m2 = col & (members - 1)
             e = jnp.where(m2 == partners[0], 0, jnp.where(m2 == partners[1], 1, 2))
             kind = kind_of(col, group, groups, members)
-            pick_ref[2 * h, s] = e
-            pick_ref[2 * h + 1, s] = jnp.where(kind == 3, 9, 3 * e + kind)
+            at = jnp.where(m2 == member, 4, rank)
+            pick_ref[2 * h, at] = e
+            pick_ref[2 * h + 1, at] = jnp.where(kind == 3, 9, 3 * e + kind)
+            if h == 0:
+                own = jnp.where(kind == 2, 3, jnp.where(kind == 3, 2, kind))
+                place_ref[0, jnp.where(m2 == member, own, 4 + rank)] = s
+            rank = rank + jnp.where(m2 == member, 0, 1)
     copies[2].wait()
     for row, out in zip(picked, (o0, o1, o2)):
         out[0:T, :] = pv[2 * row]
@@ -127,7 +132,7 @@
         out[e, :, T : 2 * T] = (block - high.astype(F32)).astype(BF)
 
 
-def local_kernel(rows, slot_ref, live_ref, dc_ref, pv, ov, dv, far_ref, q_ref, pt, aq, z):
+def local_kernel(rows, slot_ref, live_ref, dc_ref, pv, ov, dv, early_ref, far_ref, q_ref, pt, aq, z):
     zero = jnp.zeros((T, T), BF)
     pt[2 * rows] = zero
     for t in range(2 * rows):
@@ -148,8 +153,9 @@
     gs = jnp.dot(lhs, local_right(rows, z), preferred_element_type=F32).astype(BF)
     for i in range(2):
         split_into(q_ref.at[i], qs[i * T : (i + 1) * T])
-    for i, (h, c) in enumerate(((1, 1), (1, 0), (2, 2), (2, 0))):
-        far_ref[i] = gs[(h - 1) * T : h * T, c * T : (c + 1) * T]
+    for out, h in ((early_ref, 1), (far_ref, 2)):
+        for i, c in enumerate((h, 0)):
+            out[i] = gs[(h - 1) * T : h * T, c * T : (c + 1) * T]
 
 
 def received(pay_refs, rd):
@@ -174,10 +180,11 @@
 def far_kernel(pick_ref, far_ref, q_ref, r0, r1, r2, s1_ref, s4_ref, rd):
     received((r0, r1, r2), rd)
     for h, out in ((2, s4_ref), (1, s1_ref)):
-        out[0] = far_ref[2 * h - 2]
-        out[1] = far_ref[2 * h - 1]
+        at = 0 if h == 1 else 2
+        for i in range(at):
+            out[i] = far_ref[i]
         for s in range(4):
-            out[2 + s] = remote_tile(pick_ref, q_ref.at[h - 1], rd, h, s).astype(BF)
+            out[at + s] = remote_tile(pick_ref, q_ref.at[h - 1], rd, h, s).astype(BF)
 
 
 def near_kernel(rows, pick_ref, slot_ref, pt, aq, z, r0, r1, r2, own_ref, rd, q_ref):
@@ -193,15 +200,24 @@
         own_ref[4 + s] = remote_tile(pick_ref, q_ref, rd, 0, s)
 
 
-def add_kernel(own_ref, a1_ref, a4_ref, out_ref):
-    out_ref[0, 0] = own_ref[0] + a1_ref[0].astype(F32) + a4_ref[0].astype(F32)
-    out_ref[0, 1] = own_ref[1]
-    out_ref[0, 2] = own_ref[2] + a1_ref[1].astype(F32)
-    out_ref[0, 3] = own_ref[3] + a4_ref[1].astype(F32)
+def add_kernel(place_ref, own_ref, e_ref, a1_ref, a4_ref, out_hbm, out, sems):
+    def write(i, tile):
+        out[i] = tile
+        copy = pltpu.make_async_copy(out.at[i], out_hbm.at[0, place_ref[0, i]], sems.at[i])
+        copy.start()
+        return copy
+
+    copies = [
+        write(0, own_ref[0] + e_ref[0].astype(F32) + a4_ref[0].astype(F32)),
+        write(1, own_ref[1]),
+        write(2, own_ref[2] + e_ref[1].astype(F32)),
+        write(3, own_ref[3] + a4_ref[1].astype(F32)),
+    ]
     for s in range(4):
-        out_ref[0, 4 + s] = (
-            own_ref[4 + s] + a1_ref[2 + s].astype(F32) + a4_ref[2 + s].astype(F32)
-        )
+        tile = own_ref[4 + s] + a1_ref[s].astype(F32) + a4_ref[2 + s].astype(F32)
+        copies.append(write(4 + s, tile))
+    for copy in copies:
+        copy.wait()
 
 
 def on_device(
@@ -241,14 +257,15 @@
         )
 
     payload = pltpu.VMEM((2 * T + HDR, T), BF)
-    *sends, pv, slot, live, dcols, chosen = call(
+    *sends, pv, slot, live, dcols, chosen, place = call(
         functools.partial(pick_kernel, groups, members, rows),
         (
             payload, payload, payload, pltpu.VMEM((2 * rows + 1, T, T), BF),
             pltpu.SMEM((3, rows), jnp.int32),
             pltpu.SMEM((2, rows), jnp.int32),
             pltpu.SMEM((4, rows), jnp.int32),
-            pltpu.SMEM((6, 4), jnp.int32),
+            pltpu.SMEM((6, 5), jnp.int32),
+            pltpu.SMEM((1, coarse_cols.shape[1]), jnp.int32),
         ),
         [hbm] * 7,
         [
@@ -256,7 +273,6 @@
             pltpu.SMEM((2, rows), jnp.int32),
             pltpu.SMEM((2, rows), jnp.int32),
             pltpu.SMEM((rows,), jnp.int32),
-            pltpu.SMEM((4, rows), jnp.int32),
             pltpu.SMEM(coarse_cols.shape[::-1], jnp.int32),
             pltpu.SemaphoreType.DMA((7,)),
         ],
@@ -276,10 +292,11 @@
     for e in (2, 1, 0):
         got[e] = inside(lax.ppermute(sends[e], "member", pairs[e]))
 
-    far, qs, pt, aq, z = call(
+    early, far, qs, pt, aq, z = call(
         functools.partial(local_kernel, rows),
         (
-            pltpu.VMEM((4, T, T), BF),
+            pltpu.VMEM((2, T, T), BF),
+            pltpu.VMEM((2, T, T), BF),
             pltpu.VMEM((2, 3, T, 2 * T), BF),
             pltpu.VMEM((2 * rows + 1, T, T), BF),
             pltpu.VMEM((rows, 3, T, T), BF),
@@ -295,11 +312,13 @@
     def along_group(x, step):
         return inside(lax.ppermute(x, "group", [(i, (i + step) % groups) for i in range(groups)]))
 
+    sooner = along_group(early, 1)
     rd = pltpu.VMEM((10, T, T), BF)
+    four = pltpu.VMEM((4, T, T), BF)
     six = pltpu.VMEM((6, T, T), BF)
     send1, send4 = call(
         far_kernel,
-        (six, six), [smem] + [vmem] * 5, [rd], 8,
+        (four, six), [smem] + [vmem] * 5, [rd], 8,
     )(chosen, far, qs, *got)
     a4 = along_group(send4, shift)
     a1 = along_group(send1, 1)
@@ -311,11 +330,12 @@
     return pl.pallas_call(
         add_kernel,
         out_shape=jax.ShapeDtypeStruct((1, 8, T, T), F32),
-        in_specs=[vmem] * 3,
-        out_specs=vmem,
+        in_specs=[smem] + [vmem] * 4,
+        out_specs=hbm,
+        scratch_shapes=[pltpu.VMEM((8, T, T), F32), pltpu.SemaphoreType.DMA((8,))],
         compiler_params=pltpu.CompilerParams(vmem_limit_bytes=8 << 20),
         name="add",
-    )(inside(own), a1, a4)
+    )(place, inside(own), sooner, a1, a4)
 
 
 def solution(mesh):

time: 30.9 us -> 30.9 us (level)
  waiting for transfers between devices: 14.1 us -> 13.3 us
  starting transfers between devices: 10.5 us -> 11.2 us
    ppermute x2 -> x3, waiting for transfers between devices: 11.7 us -> 10.9 us  [along_group(): lax.ppermute(x, 'group', [(i, (i + step) % groups) for i in range(groups)])]
    ppermute x2 -> x3, starting transfers between devices: 7.72 us -> 8.47 us  [along_group(): lax.ppermute(x, 'group', [(i, (i + step) % groups) for i in range(groups)])]
  transfers between devices with their start and end apart: 5 -> 6, of which waited for: 3 -> 2; matrix products, arithmetic and copies ran while one was open for 0% -> 0% of each run, Pallas kernels for 12% -> 11%
where the time goes in v2:
time: 30.9 us
  waiting for transfers between devices  13.3 us (43%)
  starting transfers between devices  11.2 us (36%)
  Pallas kernels  6.31 us (20%)
    ppermute x3, waiting for transfers between devices, along_group(): lax.ppermute(x, 'group', [(i, (i + step) % groups) for i in range(groups)])  10.9 us
    ppermute x3, starting transfers between devices, along_group(): lax.ppermute(x, 'group', [(i, (i + step) % groups) for i in range(groups)])  8.47 us
    pallas_call x1, Pallas kernels, on_device(): call(functools.partial(local_kernel, rows), (pltpu.VMEM((2, T, T), BF), p...  2.74 us
    ppermute x3, starting transfers between devices, on_device(): got[e] = inside(lax.ppermute(sends[e], 'member', pairs[e]))  2.74 us
    ppermute x3, waiting for transfers between devices, on_device(): got[e] = inside(lax.ppermute(sends[e], 'member', pairs[e]))  2.36 us
    pallas_call x1, Pallas kernels, on_device(): call(functools.partial(pick_kernel, groups, members, rows), (payload, pay...  1.52 us
    pallas_call x1, Pallas kernels, on_device(): pl.pallas_call(add_kernel, out_shape=jax.ShapeDtypeStruct((1, 8, T, T), F...  0.86 us
    pallas_call x1, Pallas kernels, on_device(): call(functools.partial(near_kernel, rows), pltpu.VMEM((8, T, T), F32), [s...  0.81 us
  transfers between devices with their start and end apart: 6, of which 2 were waited for; matrix products, arithmetic and copies ran while one was open for 0% of the time, Pallas kernels for 11%

profile of v2, /device:TPU:31, one launch (start us, length us, event | category | flops | bytes accessed | tf_op | source)
XLA Modules:
  0.0 30.9 jit_solution(17040395627821018033)
XLA Ops:
  0.0 0.0 copy-start
  0.0 0.0 copy-start.1
  0.0 1.5 %shard_map.91 = (bf16[288,128]{1,0:T(8,128)(2,1)S(1)}, bf16[288,128]{1,0:T(8,128)(2,1)S(1)}, bf16[288,128]{1,0:T(8,128)(2,1)S(1)}, bf16[33,128,128]{2,1,0:T(8,12...) custom-call(s32[1,32]{1,0:T(1,128)} %bitcast.11, ...), custom_call_target="tpu_custom_call" | custom-call | flops 2000000000 | bytes 20000000 | tf_op jit(solution)/shard_map/pallas_call | solution.py:260
  1.5 0.8 %collective-permute-start = (bf16[288,128]{1,0:T(8,128)(2,1)S(1)}, bf16[288,128]{1,0:T(8,128)(2,1)S(1)}, u32[]{:S(2)}, u32[]{:S(2)}) collective-permute-start(bf16[288,128]{1,0:T(8,128)(2,1)S(1)} %get-tuple-element.31), channel_id=1, source_target_pairs={{0,1},{1,0},{2,3},{3,2},{4,5},{5,4},{6,7},{7,6},{8,9},{9,8},{10,11... | collective-permute-start | bytes 221192 | tf_op jit(solution)/shard_map/ppermute | solution.py:293
  2.3 1.5 %collective-permute-start.1 = (bf16[288,128]{1,0:T(8,128)(2,1)S(1)}, bf16[288,128]{1,0:T(8,128)(2,1)S(1)}, u32[]{:S(2)}, u32[]{:S(2)}) collective-permute-start(bf16[288,128]{1,0:T(8,128)(2,1)S(1)} %get-tuple-element.32), channel_id=1, source_target_pairs={{0,31},{1,2},{2,1},{3,4},{4,3},{5,6},{6,5},{7,8},{8,7},{9,10},{10,... | collective-permute-start | bytes 221192 | tf_op jit(solution)/shard_map/ppermute | solution.py:293
  3.8 0.4 %collective-permute-start.2 = (bf16[288,128]{1,0:T(8,128)(2,1)S(1)}, bf16[288,128]{1,0:T(8,128)(2,1)S(1)}, u32[]{:S(2)}, u32[]{:S(2)}) collective-permute-start(bf16[288,128]{1,0:T(8,128)(2,1)S(1)} %get-tuple-element.33), channel_id=1, source_target_pairs={{0,16},{1,17},{2,18},{3,19},{4,20},{5,21},{6,22},{7,23},{8,24},{9,... | collective-permute-start | bytes 221192 | tf_op jit(solution)/shard_map/ppermute | solution.py:293
  4.3 0.0 copy-done
  4.3 0.0 copy-done.1
  4.3 2.7 %shard_map.92 = (bf16[2,128,128]{2,1,0:T(8,128)(2,1)S(1)}, bf16[2,128,128]{2,1,0:T(8,128)(2,1)S(1)}, bf16[2,3,128,256]{3,2,1,0:T(8,128)(2,1)S(1)}, bf16[33,128,1...) custom-call(s32[3,16]{1,0:T(4,128)S(4)} %get-tuple-element.24.slot_ref, ...), custom_call_target="tpu_custom_call" | custom-call | flops 2000000000 | bytes 20000000 | tf_op jit(solution)/shard_map/pallas_call | solution.py:295
  7.0 0.0 collective-permute-done.r0
  7.0 2.4 %collective-permute-done.1.r1 = bf16[288,128]{1,0:T(8,128)(2,1)S(1)} collective-permute-done((bf16[288,128]{1,0:T(8,128)(2,1)S(1)}, bf16[288,128]{1,0:T(8,128)(2,1)S(1)}, u32[]{:S(2)}, u32[]{:S(2)}) %collective-permute-start.1) | collective-permute-done | bytes 73760 | tf_op jit(solution)/shard_map/ppermute | solution.py:293
  9.4 0.0 collective-permute-done.2.r2
  9.4 0.4 %shard_map.94 = (bf16[4,128,128]{2,1,0:T(8,128)(2,1)S(1)}, bf16[6,128,128]{2,1,0:T(8,128)(2,1)S(1)}) custom-call(s32[6,5]{1,0:T(8,128)S(4)} %get-tuple-element.23.pick_ref, bf16[2,128,128]{2,1,0:T(8,128)(2,1)S(1)} %get-tuple-element.35.far_ref, bf16[2,3,128,256]{3,2,1,0:T(8,128)(2,1)S(1)} %get-tuple-element.36.q_ref, ...), custom_call_target="tpu_custom_call" | custom-call | flops 10000000 | bytes 100000 | tf_op jit(solution)/shard_map/pallas_call | solution.py:319
  9.8 7.0 %collective-permute-start.5 = (bf16[6,128,128]{2,1,0:T(8,128)(2,1)S(1)}, bf16[6,128,128]{2,1,0:T(8,128)(2,1)S(1)}, u32[]{:S(2)}, u32[]{:S(2)}) collective-permute-start(bf16[6,128,128]{2,1,0:T(8,128)(2,1)S(1)} %get-tuple-element.38), channel_id=1, source_target_pairs={{0,128},{32,160},{64,192},{96,224},{128,0},{160,32},{192,64},{224,... | collective-permute-start | bytes 589832 | tf_op jit(solution)/shard_map/ppermute | solution.py:313
  16.8 0.7 %collective-permute-start.4 = (bf16[4,128,128]{2,1,0:T(8,128)(2,1)S(1)}, bf16[4,128,128]{2,1,0:T(8,128)(2,1)S(1)}, u32[]{:S(2)}, u32[]{:S(2)}) collective-permute-start(bf16[4,128,128]{2,1,0:T(8,128)(2,1)S(1)} %get-tuple-element.37), channel_id=1, source_target_pairs={{0,32},{32,64},{64,96},{96,128},{128,160},{160,192},{192,224},{224... | collective-permute-start | bytes 393224 | tf_op jit(solution)/shard_map/ppermute | solution.py:313
  17.5 0.7 %collective-permute-start.3 = (bf16[2,128,128]{2,1,0:T(8,128)(2,1)S(1)}, bf16[2,128,128]{2,1,0:T(8,128)(2,1)S(1)}, u32[]{:S(2)}, u32[]{:S(2)}) collective-permute-start(bf16[2,128,128]{2,1,0:T(8,128)(2,1)S(1)} %get-tuple-element.34), channel_id=1, source_target_pairs={{0,32},{32,64},{64,96},{96,128},{128,160},{160,192},{192,224},{224... | collective-permute-start | bytes 196616 | tf_op jit(solution)/shard_map/ppermute | solution.py:313
  18.3 0.8 %shard_map.93.own_ref = f32[8,128,128]{2,1,0:T(8,128)S(1)} custom-call(s32[6,5]{1,0:T(8,128)S(4)} %get-tuple-element.23.pick_ref, s32[3,16]{1,0:T(4,128)S(4)} %get-tuple-element.24.slot_ref, bf16[33,128,128]{2,1,0:T(8,128)(2,1)S(1)} %get-tuple-element.28.pt, bf16[16,3,128,128]{3,2,1,0:T(8,128)(2,1)S(1)} %get-tuple-element.29.aq, ...), custom_call_target="tpu_custom_call" | custom-call | flops 1000000000 | bytes 10000000 | tf_op jit(solution)/shard_map/pallas_call | solution.py:325
  19.1 10.9 %collective-permute-done.3.e_ref = bf16[2,128,128]{2,1,0:T(8,128)(2,1)S(1)} collective-permute-done((bf16[2,128,128]{2,1,0:T(8,128)(2,1)S(1)}, bf16[2,128,128]{2,1,0:T(8,128)(2,1)S(1)}, u32[]{:S(2)}, u32[]{:S(2)}) %collective-permute-start.3) | collective-permute-done | bytes 65568 | tf_op jit(solution)/shard_map/ppermute | solution.py:313
  30.0 0.0 collective-permute-done.4.a1_ref
  30.0 0.0 collective-permute-done.5.a4_ref
  30.0 0.9 %add.1 = f32[1,8,128,128]{3,2,1,0:T(8,128)} custom-call(s32[1,8]{1,0:T(1,128)S(4)} %get-tuple-element.22.place_ref, f32[8,128,128]{2,1,0:T(8,128)S(1)} %shard_map.93.own_ref, bf16[2,128,128]{2,1,0:T(8,128)(2,1)S(1)} %collective-permute-done.3.e_ref, bf16[4,128,128]{2,1,0:T(8,128)(2,1)S(1)} %collective-permute-done.4.a1_ref, ...), custom_call_target="tpu_custom_call" | custom-call | tf_op jit(solution)/shard_map/add/pallas_call | solution.py:330
Async XLA Ops:
  0.0 4.3 %copy-start = (bf16[16,4,128,128]{3,2,1,0:T(8,128)(2,1)S(1)}, bf16[16,4,128,128]{3,2,1,0:T(8,128)(2,1)}, u32[]{:S(2)}) copy-start(bf16[16,4,128,128]{3,2,1,0:T(8,128)(2,1)} %dv.1) | copy-start | bytes 6291460
  0.0 4.3 %copy-start.1 = (bf16[16,2,128,128]{3,2,1,0:T(8,128)(2,1)S(1)}, bf16[16,2,128,128]{3,2,1,0:T(8,128)(2,1)}, u32[]{:S(2)}) copy-start(bf16[16,2,128,128]{3,2,1,0:T(8,128)(2,1)} %ov.1) | copy-start | bytes 3145732
  1.5 5.5 %collective-permute-start = (bf16[288,128]{1,0:T(8,128)(2,1)S(1)}, bf16[288,128]{1,0:T(8,128)(2,1)S(1)}, u32[]{:S(2)}, u32[]{:S(2)}) collective-permute-start(bf16[288,128]{1,0:T(8,128)(2,1)S(1)} %get-tuple-element.31), channel_id=1, source_target_pairs={{0,1},{1,0},{2,3},{3,2},{4,5},{5,4},{6,7},{7,6},{8,9},{9,8},{10,11... | collective-permute-start | bytes 221192 | tf_op jit(solution)/shard_map/ppermute | solution.py:293
  2.3 7.1 %collective-permute-start.1 = (bf16[288,128]{1,0:T(8,128)(2,1)S(1)}, bf16[288,128]{1,0:T(8,128)(2,1)S(1)}, u32[]{:S(2)}, u32[]{:S(2)}) collective-permute-start(bf16[288,128]{1,0:T(8,128)(2,1)S(1)} %get-tuple-element.32), channel_id=1, source_target_pairs={{0,31},{1,2},{2,1},{3,4},{4,3},{5,6},{6,5},{7,8},{8,7},{9,10},{10,... | collective-permute-start | bytes 221192 | tf_op jit(solution)/shard_map/ppermute | solution.py:293
  3.8 5.6 %collective-permute-start.2 = (bf16[288,128]{1,0:T(8,128)(2,1)S(1)}, bf16[288,128]{1,0:T(8,128)(2,1)S(1)}, u32[]{:S(2)}, u32[]{:S(2)}) collective-permute-start(bf16[288,128]{1,0:T(8,128)(2,1)S(1)} %get-tuple-element.33), channel_id=1, source_target_pairs={{0,16},{1,17},{2,18},{3,19},{4,20},{5,21},{6,22},{7,23},{8,24},{9,... | collective-permute-start | bytes 221192 | tf_op jit(solution)/shard_map/ppermute | solution.py:293
  9.8 20.2 %collective-permute-start.5 = (bf16[6,128,128]{2,1,0:T(8,128)(2,1)S(1)}, bf16[6,128,128]{2,1,0:T(8,128)(2,1)S(1)}, u32[]{:S(2)}, u32[]{:S(2)}) collective-permute-start(bf16[6,128,128]{2,1,0:T(8,128)(2,1)S(1)} %get-tuple-element.38), channel_id=1, source_target_pairs={{0,128},{32,160},{64,192},{96,224},{128,0},{160,32},{192,64},{224,... | collective-permute-start | bytes 589832 | tf_op jit(solution)/shard_map/ppermute | solution.py:313
  16.8 13.2 %collective-permute-start.4 = (bf16[4,128,128]{2,1,0:T(8,128)(2,1)S(1)}, bf16[4,128,128]{2,1,0:T(8,128)(2,1)S(1)}, u32[]{:S(2)}, u32[]{:S(2)}) collective-permute-start(bf16[4,128,128]{2,1,0:T(8,128)(2,1)S(1)} %get-tuple-element.37), channel_id=1, source_target_pairs={{0,32},{32,64},{64,96},{96,128},{128,160},{160,192},{192,224},{224... | collective-permute-start | bytes 393224 | tf_op jit(solution)/shard_map/ppermute | solution.py:313
  17.5 12.5 %collective-permute-start.3 = (bf16[2,128,128]{2,1,0:T(8,128)(2,1)S(1)}, bf16[2,128,128]{2,1,0:T(8,128)(2,1)S(1)}, u32[]{:S(2)}, u32[]{:S(2)}) collective-permute-start(bf16[2,128,128]{2,1,0:T(8,128)(2,1)S(1)} %get-tuple-element.34), channel_id=1, source_target_pairs={{0,32},{32,64},{64,96},{96,128},{128,160},{160,192},{192,224},{224... | collective-permute-start | bytes 196616 | tf_op jit(solution)/shard_map/ppermute | solution.py:313
